TPU v7x, 32 devices: a whole 2x2x4 slice. The times are simulated.
32 devices in a mesh: parts: 2 (over y), expert: 8 (over z, x), group: 1, tensor: 2 (over core).
Axes of the slice: x: 2, y: 2, z: 4, core: 2. Of those that a mesh axis runs over, the one named last changes fastest.
Arguments:
- hidden_in: bfloat16 [3, 64, 4096], P(None, ('parts', 'expert', 'group')), parts along dimension 1, may hold values from -6 to 6
- queries: bfloat16 [3, 64, 32, 128], P(None, ('parts', 'expert', 'group'), 'tensor'), parts along dimension 1, may hold values from -32 to 32
- new_keys: bfloat16 [3, 64, 4, 128], P(None, ('parts', 'expert', 'group'), 'tensor'), parts along dimension 1, may hold values from -4 to 4
- new_values: bfloat16 [3, 64, 4, 128], P(None, ('parts', 'expert', 'group'), 'tensor'), parts along dimension 1, may hold values from -8 to 8
- cache_keys: bfloat16 [64, 4, 128, 128], P(('parts', 'expert', 'group'), 'tensor'), parts along dimension 0, may hold values from -4 to 4
- cache_values: bfloat16 [64, 4, 128, 128], P(('parts', 'expert', 'group'), 'tensor'), parts along dimension 0, may hold values from -8 to 8
- route_ids: int32 [3, 64, 8], P(None, ('parts', 'expert', 'group')), parts along dimension 1, may hold values from 0 to 15, all different within a row; in each aligned block of 4 rows (0 to 3, 4 to 7, ..., all dimensions but the last counted through in order) at most 4 rows name the same one
- route_weights: float32 [3, 64, 8], P(None, ('parts', 'expert', 'group')), parts along dimension 1, may hold values from 0.1 to 1
- norm_gain: float32 [4096], replicated, may hold values from 0.25 to 1.75
- gate_weight: bfloat16 [16, 4096, 768], P('expert', 'group', 'tensor'), may hold values from -0.09375 to 0.09375
- up_weight: bfloat16 [16, 4096, 768], P('expert', 'group', 'tensor'), may hold values from -0.09375 to 0.09375
- down_weight: bfloat16 [16, 768, 4096], P('expert', None, ('group', 'tensor')), may hold values from -0.21875 to 0.21875
- ancestor_counts: int32 [64], P(('parts', 'expert', 'group')), parts along dimension 0, may hold values from 0 to 5, as said below
Outputs:
- layer_out: bfloat16 [3, 64, 4096], P(None, ('parts', 'expert', 'group')), parts along dimension 1
- resampled_keys: bfloat16 [64, 4, 131, 128], P(('parts', 'expert', 'group'), 'tensor'), parts along dimension 0
- resampled_values: bfloat16 [64, 4, 131, 128], P(('parts', 'expert', 'group'), 'tensor'), parts along dimension 0
There are 2 independent parts, one for each index of `parts`. A program takes and returns all parts, laid end to end along the dimension named above; an argument that names none is the same for every part. Nothing has to cross between parts.
Inputs may be any that keep to these rules, and one draw needn't show every extreme that they name: `route_ids`: each row names 8 different experts; in each aligned block of 4 rows (the rows of one device in one step) no expert is named by more than 4 rows. `ancestor_counts`: the counts sum to 32, and every particle i descends from a particle within 2 positions of i.
All inputs are finite; a program needn't handle non-finite values.
Results may differ from a plain program's by a relative error of at most 0.0075.
Values may be sent and summed in bfloat16 or wider, within the bound.
A program may use at most 64 MiB of HBM per device.

v0:
```python
import math
import jax
import jax.numpy as jnp
from jax import lax
from jax.sharding import PartitionSpec as P

REACH = 2
epsilon = 1e-06
highest = lax.Precision.HIGHEST


def padded(cells, sides, width):
    for axis, dim in sides:
        count = lax.axis_size(axis)
        ends = count - 1
        head = lax.slice_in_dim(cells, 0, width, axis=dim)
        tail = lax.slice_in_dim(cells, cells.shape[dim] - width, cells.shape[dim], axis=dim)
        cells = jnp.concatenate(
            [
                lax.ppermute(tail, axis, [(i, (i + 1) % count) for i in range(ends)]),
                cells,
                lax.ppermute(head, axis, [((i + 1) % count, i) for i in range(ends)]),
            ],
            axis=dim,
        )
    return cells


def grouped_shards(
    hidden_in,
    queries,
    new_keys,
    new_values,
    cache_keys,
    cache_values,
    route_ids,
    route_weights,
    norm_gain,
    gate_weight,
    up_weight,
    down_weight,
    ancestor_counts,
):
    step_count, token_count, query_heads, head_width = queries.shape
    key_heads = cache_keys.shape[1]
    cached = cache_keys.shape[2]
    group_size = query_heads // key_heads
    cache_pair = jnp.stack([cache_keys, cache_values])
    fresh_pair = jnp.transpose(jnp.stack([new_keys, new_values]), (0, 2, 3, 1, 4))
    both_kv = jnp.concatenate([cache_pair, fresh_pair], axis=3)
    length = both_kv.shape[3]
    grouped = queries.reshape(step_count, token_count, key_heads, group_size, head_width)
    scores = jnp.einsum(
        "sphgd,phld->sphgl", grouped, both_kv[0], preferred_element_type=jnp.float32
    ) / math.sqrt(head_width)
    allowed = lax.broadcasted_iota(
        jnp.int32, (step_count, length), 1
    ) <= cached + lax.broadcasted_iota(jnp.int32, (step_count, length), 0)
    scores = jnp.where(allowed[:, None, None, None, :], scores, -1e30)
    exponent = jnp.exp(scores - jnp.max(scores, axis=-1, keepdims=True))
    attn_weights = (exponent / jnp.sum(exponent, axis=-1, keepdims=True)).astype(jnp.bfloat16)
    attended = jnp.einsum(
        "sphgl,phld->sphgd", attn_weights, both_kv[1], preferred_element_type=jnp.float32
    )
    attended = attended.astype(jnp.bfloat16).reshape(
        step_count, token_count, query_heads * head_width
    )
    attended = lax.all_gather(attended, "tensor", axis=2, tiled=True)
    expert_count = lax.axis_size("expert")
    group_count = lax.axis_size("group")
    tensor_count = lax.axis_size("tensor")
    tensor_index = lax.axis_index("tensor")
    expert_local = gate_weight.shape[0]
    experts_all = expert_local * expert_count
    chosen_count = route_ids.shape[2]
    model_width = hidden_in.shape[2]
    column_width = down_weight.shape[2]
    capacity = min(token_count, max(2, 2 * token_count * chosen_count // experts_all))
    pair_count = token_count * chosen_count
    expert_iota = jnp.arange(experts_all, dtype=jnp.int32)
    slot_iota = jnp.arange(capacity, dtype=jnp.int32)
    token_owner = (
        (jnp.arange(pair_count) // chosen_count)[:, None] == jnp.arange(token_count)[None, :]
    ).astype(jnp.float32)
    halves = []
    for step_index in range(step_count):
        residual = hidden_in[step_index].astype(jnp.float32) + attended[step_index].astype(
            jnp.float32
        )
        normed = (
            residual
            * lax.rsqrt(jnp.mean(residual * residual, axis=-1, keepdims=True) + epsilon)
            * norm_gain
        ).astype(jnp.bfloat16)
        chosen = route_ids[step_index].reshape(pair_count)
        route_share = route_weights[step_index] / jnp.sum(
            route_weights[step_index], axis=-1, keepdims=True
        )
        expert_hits = (chosen[:, None] == expert_iota[None, :]).astype(jnp.int32)
        position = jnp.sum((jnp.cumsum(expert_hits, axis=0) - expert_hits) * expert_hits, axis=1)
        slotted = (
            expert_hits[:, :, None]
            * (position[:, None, None] == slot_iota[None, None, :]).astype(jnp.int32)
        ).astype(jnp.float32)
        dispatch = jnp.einsum("rec,rt->ect", slotted, token_owner, precision=highest)
        dispatch = dispatch.reshape(expert_count, expert_local, capacity, token_count).astype(
            jnp.bfloat16
        )
        combine = jnp.einsum(
            "rec,rt,r->tec",
            slotted,
            token_owner,
            route_share.reshape(pair_count),
            precision=highest,
        )
        combine = combine.reshape(token_count, expert_count, expert_local, capacity)
        feature_blocks = normed.reshape(token_count, group_count, model_width // group_count)
        outgoing = jnp.einsum(
            "aict,tgd->agicd", dispatch, feature_blocks, preferred_element_type=jnp.float32
        ).astype(jnp.bfloat16)
        flattened = outgoing.reshape(
            expert_count * group_count, expert_local, capacity, model_width // group_count
        )
        received = lax.all_to_all(
            flattened, ("expert", "group"), split_axis=0, concat_axis=0, tiled=True
        )
        gate_part = jnp.einsum(
            "seki,eif->sekf", received, gate_weight, preferred_element_type=jnp.float32
        ).astype(jnp.bfloat16)
        up_part = jnp.einsum(
            "seki,eif->sekf", received, up_weight, preferred_element_type=jnp.float32
        ).astype(jnp.bfloat16)
        gate_sum = lax.psum(gate_part, "group").astype(jnp.float32)
        up_sum = lax.psum(up_part, "group").astype(jnp.float32)
        hidden = (jax.nn.silu(gate_sum) * up_sum).astype(jnp.bfloat16)
        hidden = lax.all_gather(hidden, "tensor", axis=3, tiled=True)
        answered = jnp.einsum(
            "sekf,efo->seko", hidden, down_weight, preferred_element_type=jnp.float32
        ).astype(jnp.bfloat16)
        returned = lax.all_to_all(
            answered, ("expert", "group"), split_axis=0, concat_axis=0, tiled=True
        )
        returned = returned.reshape(
            expert_count, group_count, expert_local, capacity, column_width
        ).astype(jnp.float32)
        expert_mix = jnp.einsum("taic,agicd->tgd", combine, returned, precision=highest)
        own_columns = lax.dynamic_index_in_dim(
            residual.reshape(token_count, group_count, tensor_count, column_width),
            tensor_index,
            2,
            keepdims=False,
        )
        halves.append((own_columns + expert_mix).astype(jnp.bfloat16))
    stacked = jnp.stack(halves)
    layer_out = lax.all_gather(stacked, "tensor", axis=3, tiled=True).reshape(
        step_count, token_count, model_width
    )
    every_count = lax.all_gather(ancestor_counts, ("expert", "group"), axis=0, tiled=True)
    running = jnp.cumsum(every_count)
    first_index = lax.axis_index(("expert", "group")) * token_count
    own_index = first_index + jnp.arange(token_count, dtype=jnp.int32)
    ancestor = jnp.sum((running[None, :] <= own_index[:, None]).astype(jnp.int32), axis=1)
    widened = padded(both_kv, ((("expert", "group"), 1),), REACH)
    window_index = first_index - REACH + jnp.arange(token_count + 2 * REACH, dtype=jnp.int32)
    selector = (ancestor[:, None] == window_index[None, :]).astype(jnp.bfloat16)
    resampled = jnp.einsum(
        "tw,kwhld->kthld", selector, widened, preferred_element_type=jnp.float32
    ).astype(jnp.bfloat16)
    return (layer_out, resampled[0], resampled[1])


def one_group_shards(
    hidden_in,
    queries,
    new_keys,
    new_values,
    cache_keys,
    cache_values,
    route_ids,
    route_weights,
    norm_gain,
    gate_weight,
    up_weight,
    down_weight,
    ancestor_counts,
):
    step_count, token_count, query_heads, head_width = queries.shape
    key_heads = cache_keys.shape[1]
    cached = cache_keys.shape[2]
    group_size = query_heads // key_heads
    rows = step_count * token_count
    model_width = hidden_in.shape[2]
    expert_count = lax.axis_size("expert")
    expert_index = lax.axis_index("expert")
    expert_local = gate_weight.shape[0]
    experts_all = expert_local * expert_count
    column_width = down_weight.shape[2]
    tensor_index = lax.axis_index("tensor")
    cache_pair = jnp.stack([cache_keys, cache_values])
    fresh_pair = jnp.transpose(jnp.stack([new_keys, new_values]), (0, 2, 3, 1, 4))
    both_kv = jnp.concatenate([cache_pair, fresh_pair], axis=3)
    length = both_kv.shape[3]
    grouped = queries.reshape(step_count, token_count, key_heads, group_size, head_width)
    scores = jnp.einsum(
        "sphgd,phld->sphgl", grouped, both_kv[0], preferred_element_type=jnp.float32
    ) / math.sqrt(head_width)
    allowed = lax.broadcasted_iota(
        jnp.int32, (step_count, length), 1
    ) <= cached + lax.broadcasted_iota(jnp.int32, (step_count, length), 0)
    scores = jnp.where(allowed[:, None, None, None, :], scores, -1e30)
    exponent = jnp.exp(scores - jnp.max(scores, axis=-1, keepdims=True))
    attn_weights = (exponent / jnp.sum(exponent, axis=-1, keepdims=True)).astype(jnp.bfloat16)
    attended = jnp.einsum(
        "sphgl,phld->sphgd", attn_weights, both_kv[1], preferred_element_type=jnp.float32
    )
    attended = attended.astype(jnp.bfloat16).reshape(rows, query_heads * head_width)
    attended = lax.all_gather(attended, "tensor", axis=1, tiled=True)
    residual = hidden_in.reshape(rows, model_width).astype(jnp.float32) + attended.astype(
        jnp.float32
    )
    normed = (
        residual
        * lax.rsqrt(jnp.mean(residual * residual, axis=-1, keepdims=True) + epsilon)
        * norm_gain
    ).astype(jnp.bfloat16)
    share = route_weights / jnp.sum(route_weights, axis=-1, keepdims=True)
    hits = route_ids[..., None] == jnp.arange(experts_all, dtype=jnp.int32)
    mix = jnp.sum(jnp.where(hits, share[..., None], 0.0), axis=2).reshape(rows, experts_all)
    counts = jnp.broadcast_to(ancestor_counts.astype(jnp.float32)[None, :], (rows, token_count))
    table = jnp.concatenate([mix, counts], axis=1)
    spare = -table.shape[1] % 128
    table = jnp.pad(table, ((0, 0), (0, spare)))
    table = lax.all_gather(table, "expert", axis=0, tiled=True)
    tokens = lax.all_gather(normed, "expert", axis=0, tiled=True)
    gate = jnp.einsum("ri,eif->erf", tokens, gate_weight, preferred_element_type=jnp.float32)
    up = jnp.einsum("ri,eif->erf", tokens, up_weight, preferred_element_type=jnp.float32)
    gate = gate.astype(jnp.bfloat16).astype(jnp.float32)
    up = up.astype(jnp.bfloat16).astype(jnp.float32)
    hidden = (jax.nn.silu(gate) * up).astype(jnp.bfloat16)
    hidden = lax.all_gather(hidden, "tensor", axis=2, tiled=True)
    answered = jnp.einsum("erf,efo->ero", hidden, down_weight, preferred_element_type=jnp.float32)
    own_mix = lax.dynamic_slice_in_dim(table, expert_index * expert_local, expert_local, axis=1)
    partial = jnp.sum(answered * own_mix.T[:, :, None], axis=0).astype(jnp.bfloat16)
    returned = lax.all_to_all(
        partial.reshape(expert_count, rows, column_width), "expert", 0, 0, tiled=True
    )
    expert_mix = jnp.sum(returned.astype(jnp.float32), axis=0)
    own_columns = lax.dynamic_slice_in_dim(
        residual, tensor_index * column_width, column_width, axis=1
    )
    half = (own_columns + expert_mix).astype(jnp.bfloat16)
    layer_out = lax.all_gather(half, "tensor", axis=1, tiled=True).reshape(
        step_count, token_count, model_width
    )
    every_count = table.reshape(expert_count, rows, -1)[
        :, 0, experts_all : experts_all + token_count
    ].reshape(-1)
    running = jnp.cumsum(every_count.astype(jnp.int32))
    first_index = expert_index * token_count
    own_index = first_index + jnp.arange(token_count, dtype=jnp.int32)
    ancestor = jnp.sum((running[None, :] <= own_index[:, None]).astype(jnp.int32), axis=1)
    widened = padded(both_kv, ((("expert", "group"), 1),), REACH)
    window_index = first_index - REACH + jnp.arange(token_count + 2 * REACH, dtype=jnp.int32)
    selector = (ancestor[:, None] == window_index[None, :]).astype(jnp.bfloat16)
    resampled = jnp.einsum(
        "tw,kwhld->kthld", selector, widened, preferred_element_type=jnp.float32
    ).astype(jnp.bfloat16)
    return (layer_out, resampled[0], resampled[1])


def solution(mesh):
    shards = one_group_shards if mesh.shape["group"] == 1 else grouped_shards
    in_specs = (
        P(None, ("parts", "expert", "group"), None),
        P(None, ("parts", "expert", "group"), "tensor", None),
        P(None, ("parts", "expert", "group"), "tensor", None),
        P(None, ("parts", "expert", "group"), "tensor", None),
        P(("parts", "expert", "group"), "tensor", None, None),
        P(("parts", "expert", "group"), "tensor", None, None),
        P(None, ("parts", "expert", "group"), None),
        P(None, ("parts", "expert", "group"), None),
        P(),
        P("expert", "group", "tensor"),
        P("expert", "group", "tensor"),
        P("expert", None, ("group", "tensor")),
        P(("parts", "expert", "group")),
    )
    out_specs = (
        P(None, ("parts", "expert", "group"), None),
        P(("parts", "expert", "group"), "tensor", None, None),
        P(("parts", "expert", "group"), "tensor", None, None),
    )
    return jax.shard_map(shards, mesh=mesh, in_specs=in_specs, out_specs=out_specs, check_vma=False)
```

profile of v0, /device:TPU:0, one launch (start us, length us, event | category | flops | bytes accessed | tf_op | source)
XLA Modules:
  0.0 117.5 jit_solution(2115568042403816963)
XLA Ops:
  0.7 0.8 copy_bitcast_fusion
  1.5 1.1 pad_maximum_fusion.1
  2.6 0.9 fusion.25
  3.4 5.0 %collective-permute-start = (bf16[2,2,2,131,128]{4,3,2,1,0:T(8,128)(2,1)}, bf16[2,2,2,131,128]{4,3,2,1,0:T(8,128)(2,1)S(1)}, u32[]{:S(2)}, u32[]{:S(2)}) collective-permute-start(bf16[2,2,2,131,128]{4,3,2,1,0:T(8,128)(2,1)} %get-tuple-element.17), channel_id=1, source_target_pairs={{0,2},{2,4},{4,6},{6,8},{8,10},{10,12},{12,14},{1,3},{3,5},{5,7},{... | collective-permute-start | bytes 804872 | tf_op jit(solution)/shard_map/ppermute | solution.py:20
  8.4 1.3 %collective-permute-start.1 = (bf16[2,2,2,131,128]{4,3,2,1,0:T(8,128)(2,1)}, bf16[2,2,2,131,128]{4,3,2,1,0:T(8,128)(2,1)}, u32[]{:S(2)}, u32[]{:S(2)}) collective-permute-start(bf16[2,2,2,131,128]{4,3,2,1,0:T(8,128)(2,1)} %get-tuple-element.18), channel_id=1, source_target_pairs={{2,0},{4,2},{6,4},{8,6},{10,8},{12,10},{14,12},{3,1},{5,3},{7,5},{... | collective-permute-start | bytes 804872 | tf_op jit(solution)/shard_map/ppermute | solution.py:22
  9.9 0.1 select_reduce_fusion
  10.2 36.5 %all-gather.1 = f32[8,12,128]{2,1,0:T(8,128)S(1)} all-gather(f32[1,12,128]{2,1,0:T(8,128)S(1)} %pad_bitcast_fusion), channel_id=1, replica_groups=mesh['parts'=2,'expert'=8,'group'=1,'tensor'=2] {'expert'}, dimensions={0}, use_global_device_ids=true | all-gather | bytes 55296 | tf_op jit(solution)/shard_map/all_gather | solution.py:233
  46.7 0.6 copy.46
  47.4 0.3 fusion.11
  47.6 0.2 fusion.26
  47.9 0.4 fusion.13
  48.3 1.9 %all_gather.15 = bf16[12,4096]{1,0:T(8,128)(2,1)S(1)} all-gather(bf16[12,2048]{1,0:T(8,128)(2,1)S(1)} %reshape.97), channel_id=1, replica_groups=mesh['parts'=2,'expert'=8,'group'=1,'tensor'=2] {'tensor'}, dimensions={1}, use_global_device_ids=true | all-gather | bytes 147456 | tf_op jit(solution)/shard_map/all_gather | solution.py:217
  50.2 0.2 multiply_reduce_fusion
  50.4 0.1 fusion.15
  50.5 34.9 %all-gather = bf16[8,12,4096]{2,1,0:T(8,128)(2,1)} all-gather(bf16[1,12,4096]{2,1,0:T(8,128)(2,1)S(1)} %fusion.15), channel_id=1, replica_groups=mesh['parts'=2,'expert'=8,'group'=1,'tensor'=2] {'expert'}, dimensions={0}, use_global_device_ids=true | all-gather | bytes 884736 | tf_op jit(solution)/shard_map/all_gather | solution.py:234
  85.4 1.5 %reshape.110 = bf16[96,4096,1]{1,0,2:T(8,128)(2,1)S(1)} reshape(bf16[8,12,4096]{2,1,0:T(8,128)(2,1)} %all-gather) | data formatting | bytes 1572864
  86.9 4.1 %fusion.9 = f32[2,96,384]{2,1,0:T(8,128)S(1)} fusion(bf16[96,4096,1]{1,0,2:T(8,128)(2,1)S(1)} %reshape.110, bf16[2,4096,384]{2,1,0:T(8,128)(2,1)} %param.22), kind=kOutput, calls=%fused_computation.13 | convolution fusion | flops 604127232 | bytes 7372800 | tf_op jit(solution)/shard_map/ri,eif->erf/dot_general | solution.py:235
  91.1 1.1 fusion.7
  92.2 2.0 %all_gather.17 = bf16[2,96,768]{2,1,0:T(8,128)(2,1)S(1)} all-gather(bf16[2,96,384]{2,1,0:T(8,128)(2,1)S(1)} %fusion.7), channel_id=1, replica_groups=mesh['parts'=2,'expert'=8,'group'=1,'tensor'=2] {'tensor'}, dimensions={2}, use_global_device_ids=true | all-gather | bytes 442368 | tf_op jit(solution)/shard_map/all_gather | solution.py:240
  94.2 1.2 fusion.1
  95.4 0.9 convert_element_type.103
  96.3 3.5 %all-to-all-start = ((bf16[8,12,2048]{2,1,0:T(8,128)(2,1)}), bf16[8,12,2048]{2,1,0:T(8,128)(2,1)S(1)}, u32[]{:S(2)}, u32[]{:S(2)}) async-start(bf16[8,12,2048]{2,1,0:T(8,128)(2,1)} %convert_element_type.103), calls=%async_computation | async-start | bytes 1048576 | tf_op jit(solution)/shard_map/all_to_all | solution.py:244
  100.0 0.1 reduce.1
  100.1 0.2 convert_reduce_fusion.1
  100.4 1.0 pad_maximum_fusion
  101.4 0.5 fusion.2
  101.9 0.2 slice_bitcast_fusion.4
  102.1 0.9 copy.50
  103.0 0.9 copy.49
  104.0 10.8 %all-to-all-done = bf16[8,12,2048]{2,1,0:T(8,128)(2,1)S(1)} async-done(((bf16[8,12,2048]{2,1,0:T(8,128)(2,1)}), bf16[8,12,2048]{2,1,0:T(8,128)(2,1)S(1)}, u32[]{:S(2)}, u32[]{:S(2)}) %all-to-all-start) | async-done | bytes 393248 | tf_op jit(solution)/shard_map/all_to_all | solution.py:244
  114.9 1.9 %all_gather.19 = bf16[12,4096]{1,0:T(8,128)(2,1)S(1)} all-gather(bf16[12,2048]{1,0:T(8,128)(2,1)S(1)} %add_convert_fusion), channel_id=1, replica_groups=mesh['parts'=2,'expert'=8,'group'=1,'tensor'=2] {'tensor'}, dimensions={1}, use_global_device_ids=true | all-gather | bytes 147456 | tf_op jit(solution)/shard_map/all_gather | solution.py:252
  116.8 0.7 reshape.99
  (52 shorter events, 0.9 us)
Async XLA Ops:
  0.6 46.7 %copy-start = (bf16[3,4,16,128]{3,2,1,0:T(8,128)(2,1)S(1)}, bf16[3,4,16,128]{3,2,1,0:T(8,128)(2,1)}, u32[]{:S(2)}) copy-start(bf16[3,4,16,128]{3,2,1,0:T(8,128)(2,1)} %param.14) | copy-start | bytes 147460
  0.6 9.1 %copy-start.8 = (s32[4]{0:T(128)S(1)}, s32[4]{0:T(128)}, u32[]{:S(2)}) copy-start(s32[4]{0:T(128)} %param.25) | copy-start | bytes 52
  0.7 9.2 %copy-start.7 = (f32[3,4,8]{2,1,0:T(4,128)S(1)}, f32[3,4,8]{2,1,0:T(4,128)}, u32[]{:S(2)}) copy-start(f32[3,4,8]{2,1,0:T(4,128)} %param.20) | copy-start | bytes 1156
  0.7 9.3 %copy-start.6 = (s32[3,4,8]{2,1,0:T(4,128)S(1)}, s32[3,4,8]{2,1,0:T(4,128)}, u32[]{:S(2)}) copy-start(s32[3,4,8]{2,1,0:T(4,128)} %param.19) | copy-start | bytes 1156
  0.7 46.7 %copy-start.3 = (bf16[3,4,4096]{2,1,0:T(4,128)(2,1)S(1)}, bf16[3,4,4096]{2,1,0:T(4,128)(2,1)}, u32[]{:S(2)}) copy-start(bf16[3,4,4096]{2,1,0:T(4,128)(2,1)} %param.13) | copy-start | bytes 294916
  3.4 47.0 %copy-start.4 = (f32[4096]{0:T(1024)S(1)}, f32[4096]{0:T(1024)}, u32[]{:S(2)}) copy-start(f32[4096]{0:T(1024)} %param.21) | copy-start | bytes 49156
  3.4 96.9 %collective-permute-start = (bf16[2,2,2,131,128]{4,3,2,1,0:T(8,128)(2,1)}, bf16[2,2,2,131,128]{4,3,2,1,0:T(8,128)(2,1)S(1)}, u32[]{:S(2)}, u32[]{:S(2)}) collective-permute-start(bf16[2,2,2,131,128]{4,3,2,1,0:T(8,128)(2,1)} %get-tuple-element.17), channel_id=1, source_target_pairs={{0,2},{2,4},{4,6},{6,8},{8,10},{10,12},{12,14},{1,3},{3,5},{5,7},{... | collective-permute-start | bytes 804872 | tf_op jit(solution)/shard_map/ppermute | solution.py:20
  8.4 91.9 %collective-permute-start.1 = (bf16[2,2,2,131,128]{4,3,2,1,0:T(8,128)(2,1)}, bf16[2,2,2,131,128]{4,3,2,1,0:T(8,128)(2,1)}, u32[]{:S(2)}, u32[]{:S(2)}) collective-permute-start(bf16[2,2,2,131,128]{4,3,2,1,0:T(8,128)(2,1)} %get-tuple-element.18), channel_id=1, source_target_pairs={{2,0},{4,2},{6,4},{8,6},{10,8},{12,10},{14,12},{3,1},{5,3},{7,5},{... | collective-permute-start | bytes 804872 | tf_op jit(solution)/shard_map/ppermute | solution.py:22
  85.4 5.6 %slice-start = ((s8[6291456]{0:T(1024)(128)(4,1)}), s8[2097152]{0:T(1024)(128)(4,1)S(1)}, s32[]{:S(2)}) async-start(s8[6291456]{0:T(1024)(128)(4,1)} %bitcast.66), calls=%async_computation.1 | async-start | bytes 4194304
  86.9 4.1 %slice-start.1 = ((s8[6291456]{0:T(1024)(128)(4,1)}), s8[4194304]{0:T(1024)(128)(4,1)S(1)}, s32[]{:S(2)}) async-start(s8[6291456]{0:T(1024)(128)(4,1)} %bitcast.66), calls=%async_computation.2 | async-start | bytes 8388608
  86.9 7.3 %slice-start.2 = ((s8[6291456]{0:T(1024)(128)(4,1)}), s8[4194304]{0:T(1024)(128)(4,1)S(1)}, s32[]{:S(2)}) async-start(s8[6291456]{0:T(1024)(128)(4,1)} %bitcast.68), calls=%async_computation.3 | async-start | bytes 8388608
  91.0 3.2 %slice-start.3 = ((s8[6291456]{0:T(1024)(128)(4,1)}), s8[2097152]{0:T(1024)(128)(4,1)S(1)}, s32[]{:S(2)}) async-start(s8[6291456]{0:T(1024)(128)(4,1)} %bitcast.68), calls=%async_computation.4 | async-start | bytes 4194304
  91.0 3.2 %copy-start.5 = (f32[2,96]{1,0:T(2,128)S(1)}, f32[2,96]{1,0:T(2,128)}, u32[]{:S(2)}) copy-start(f32[2,96]{1,0:T(2,128)} %copy.46) | copy-start | bytes 2308
  95.4 5.0 %copy-start.1 = (bf16[4,2,128,128]{3,2,1,0:T(8,128)(2,1)S(1)}, bf16[4,2,128,128]{3,2,1,0:T(8,128)(2,1)}, u32[]{:S(2)}) copy-start(bf16[4,2,128,128]{3,2,1,0:T(8,128)(2,1)} %param.18) | copy-start | bytes 786436
  95.4 5.0 %copy-start.2 = (bf16[4,2,128,128]{3,2,1,0:T(8,128)(2,1)S(1)}, bf16[4,2,128,128]{3,2,1,0:T(8,128)(2,1)}, u32[]{:S(2)}) copy-start(bf16[4,2,128,128]{3,2,1,0:T(8,128)(2,1)} %param.17) | copy-start | bytes 786436
  96.3 18.5 %all-to-all-start = ((bf16[8,12,2048]{2,1,0:T(8,128)(2,1)}), bf16[8,12,2048]{2,1,0:T(8,128)(2,1)S(1)}, u32[]{:S(2)}, u32[]{:S(2)}) async-start(bf16[8,12,2048]{2,1,0:T(8,128)(2,1)} %convert_element_type.103), calls=%async_computation | async-start | bytes 1048576 | tf_op jit(solution)/shard_map/all_to_all | solution.py:244
where the time goes:
time: 118 us; the launch traced here: 117 us
  blocking collectives  77.2 us (65%)
  waiting for transfers between devices  10.8 us (9%)
  starting transfers between devices  9.79 us (8%)
  local copies, waits for them, and re-layouts  7.75 us (7%)
  matrix products  7.53 us (6%)
  other arithmetic  3.44 us (3%)
    all_gather x1, blocking collectives, one_group_shards(): table = lax.all_gather(table, 'expert', axis=0, tiled=True)  36.5 us
    all_gather x1, blocking collectives, one_group_shards(): tokens = lax.all_gather(normed, 'expert', axis=0, tiled=True)  34.9 us
    all_to_all x1, waiting for transfers between devices, one_group_shards(): lax.all_to_all(partial.reshape(expert_count, rows, column_width), 'expert...  10.8 us
    ppermute x1, starting transfers between devices, padded(): lax.ppermute(tail, axis, [(i, (i + 1) % count) for i in range(ends)])  5.01 us
    dot_general x1, matrix products, one_group_shards(): jnp.einsum('ri,eif->erf', tokens, gate_weight, preferred_element_type=jnp...  4.06 us
    all_to_all x1, starting transfers between devices, one_group_shards(): lax.all_to_all(partial.reshape(expert_count, rows, column_width), 'expert...  3.49 us
    unnamed x31, local copies, waits for them, and re-layouts  3.42 us
  transfers between devices with their start and end apart: 3, of which 1 were waited for; matrix products, arithmetic and copies ran while one was open for 13% of the time, Pallas kernels for 0%

commit v1 on v0

--- a/solution.py
+++ b/solution.py
@@ -230,8 +230,11 @@
     table = jnp.concatenate([mix, counts], axis=1)
     spare = -table.shape[1] % 128
     table = jnp.pad(table, ((0, 0), (0, spare)))
-    table = lax.all_gather(table, "expert", axis=0, tiled=True)
-    tokens = lax.all_gather(normed, "expert", axis=0, tiled=True)
+    table, tokens = jnp.split(
+        lax.all_gather(jnp.concatenate([table, normed], axis=1), "expert", axis=0, tiled=True),
+        [table.shape[1]],
+        axis=1,
+    )
     gate = jnp.einsum("ri,eif->erf", tokens, gate_weight, preferred_element_type=jnp.float32)
     up = jnp.einsum("ri,eif->erf", tokens, up_weight, preferred_element_type=jnp.float32)
     gate = gate.astype(jnp.bfloat16).astype(jnp.float32)

time: 118 us -> 115 us (0.975)
  blocking collectives: 77.2 us -> 5.96 us
  waiting for transfers between devices: 10.8 us -> 62 us
  between operations: 0.98 us -> 14.3 us
  matrix products: 7.53 us -> 13 us
  local copies, waits for them, and re-layouts: 7.75 us -> 6.43 us
    all_gather x2 -> x0, blocking collectives: 71.3 us -> none  [the longest x1 36.5 us: one_group_shards(): table = lax.all_gather(table, 'expert', axis=0, tiled=True)]
    all_gather x0 -> x1, waiting for transfers between devices: none -> 37 us  [one_group_shards(): lax.all_gather(jnp.concatenate([table, normed], axis=1), 'expert', axis=0...]
    ppermute x1, waiting for transfers between devices: 0.01 us -> 13.1 us  [padded(): lax.ppermute(tail, axis, [(i, (i + 1) % count) for i in range(ends)])]
    dot_general x1, matrix products: 1.16 us -> 3.98 us  [one_group_shards(): jnp.einsum('erf,efo->ero', hidden, down_weight, preferred_element_type=jn...]
    dot_general x1, matrix products: 1.14 us -> 3.93 us  [one_group_shards(): jnp.einsum('ri,eif->erf', tokens, up_weight, preferred_element_type=jnp.f...]
    unnamed x31 -> x19, local copies, waits for them, and re-layouts: 3.42 us -> 3.53 us
  transfers between devices with their start and end apart: 3 -> 4, of which waited for: 1 -> 3; matrix products, arithmetic and copies ran while one was open for 13% -> 3% of each run, Pallas kernels for 0% -> 0%
where the time goes in v1:
time: 115 us
  waiting for transfers between devices  62 us (54%)
  between operations  14.3 us (12%)
  matrix products  13 us (11%)
  starting transfers between devices  9.57 us (8%)
  local copies, waits for them, and re-layouts  6.43 us (6%)
  blocking collectives  5.96 us (5%)
  other arithmetic  3.25 us (3%)
    all_gather x1, waiting for transfers between devices, one_group_shards(): lax.all_gather(jnp.concatenate([table, normed], axis=1), 'expert', axis=0...  37 us
    ppermute x1, waiting for transfers between devices, padded(): lax.ppermute(tail, axis, [(i, (i + 1) % count) for i in range(ends)])  13.1 us
    all_to_all x1, waiting for transfers between devices, one_group_shards(): lax.all_to_all(partial.reshape(expert_count, rows, column_width), 'expert...  11.9 us
    ppermute x1, starting transfers between devices, padded(): lax.ppermute(tail, axis, [(i, (i + 1) % count) for i in range(ends)])  4.75 us
    dot_general x1, matrix products, one_group_shards(): jnp.einsum('erf,efo->ero', hidden, down_weight, preferred_element_type=jn...  3.98 us
    dot_general x1, matrix products, one_group_shards(): jnp.einsum('ri,eif->erf', tokens, up_weight, preferred_element_type=jnp.f...  3.93 us
    dot_general x1, matrix products, one_group_shards(): jnp.einsum('ri,eif->erf', tokens, gate_weight, preferred_element_type=jnp...  3.91 us
    unnamed x19, local copies, waits for them, and re-layouts  3.53 us
  transfers between devices with their start and end apart: 4, of which 3 were waited for; matrix products, arithmetic and copies ran while one was open for 3% of the time, Pallas kernels for 0%

profile of v1, /device:TPU:0, one launch (start us, length us, event | category | flops | bytes accessed | tf_op | source)
XLA Modules:
  0.0 114.6 jit_solution(5811231508816310243)
XLA Ops:
  7.3 0.7 copy_bitcast_fusion
  8.1 1.1 pad_maximum_fusion.1
  9.2 0.3 fusion.15
  9.5 0.2 fusion.31
  9.7 0.4 fusion.17
  10.2 2.0 %all_gather.12 = bf16[12,4096]{1,0:T(8,128)(2,1)S(1)} all-gather(bf16[12,2048]{1,0:T(8,128)(2,1)S(1)} %reshape.97), channel_id=1, replica_groups=mesh['parts'=2,'expert'=8,'group'=1,'tensor'=2] {'tensor'}, dimensions={1}, use_global_device_ids=true | all-gather | bytes 147456 | tf_op jit(solution)/shard_map/all_gather | solution.py:217
  12.3 0.2 multiply_reduce_fusion
  12.5 0.1 select_reduce_fusion
  12.8 0.1 fusion.20
  12.9 0.7 fusion.19
  13.7 4.8 %collective-permute-start = (bf16[2,2,2,131,128]{4,3,2,1,0:T(8,128)(2,1)S(1)}, bf16[2,2,2,131,128]{4,3,2,1,0:T(8,128)(2,1)S(1)}, u32[]{:S(2)}, u32[]{:S(2)}) collective-permute-start(bf16[2,2,2,131,128]{4,3,2,1,0:T(8,128)(2,1)S(1)} %get-tuple-element.17), channel_id=1, source_target_pairs={{0,2},{2,4},{4,6},{6,8},{8,10},{10,12},{12,14},{1,3},{3,5},{5,7},{... | collective-permute-start | bytes 804872 | tf_op jit(solution)/shard_map/ppermute | solution.py:20
  18.4 1.3 %collective-permute-start.1 = (bf16[2,2,2,131,128]{4,3,2,1,0:T(8,128)(2,1)S(1)}, bf16[2,2,2,131,128]{4,3,2,1,0:T(8,128)(2,1)S(1)}, u32[]{:S(2)}, u32[]{:S(2)}) collective-permute-start(bf16[2,2,2,131,128]{4,3,2,1,0:T(8,128)(2,1)S(1)} %get-tuple-element.18), channel_id=1, source_target_pairs={{2,0},{4,2},{6,4},{8,6},{10,8},{12,10},{14,12},{3,1},{5,3},{7,5},{... | collective-permute-start | bytes 804872 | tf_op jit(solution)/shard_map/ppermute | solution.py:22
  19.8 13.1 %collective-permute-done = bf16[2,2,2,131,128]{4,3,2,1,0:T(8,128)(2,1)S(1)} collective-permute-done((bf16[2,2,2,131,128]{4,3,2,1,0:T(8,128)(2,1)S(1)}, bf16[2,2,2,131,128]{4,3,2,1,0:T(8,128)(2,1)S(1)}, u32[]{:S(2)}, u32[]{:S(2)}) %collective-permute-start) | collective-permute-done | bytes 268320 | tf_op jit(solution)/shard_map/ppermute | solution.py:20
  33.0 37.0 %all-gather.3.cloned.1.call-done = f32[8,12,4224]{2,1,0:T(8,128)} async-done(((f32[1,12,4224]{2,1,0:T(8,128)}), f32[8,12,4224]{2,1,0:T(8,128)}) %all-gather.3.cloned.1.call-update) | async-done | bytes 1622032 | tf_op jit(solution)/shard_map/all_gather | solution.py:234
  70.0 1.7 %reshape.104 = f32[96,4224]{1,0:T(8,128)S(1)} reshape(f32[8,12,4224]{2,1,0:T(8,128)} %all-gather.3.cloned.1.call-done) | data formatting | bytes 3244032
  71.6 3.9 %fusion.8 = f32[2,96,384]{2,1,0:T(8,128)S(1)} fusion(bf16[2,4096,384]{2,1,0:T(8,128)(2,1)} %param.22, f32[96,4224]{1,0:T(8,128)S(1)} %reshape.104), kind=kOutput, calls=%fused_computation.11 | convolution fusion | flops 604053504 | bytes 7372800 | tf_op jit(solution)/shard_map/ri,eif->erf/dot_general | solution.py:238
  75.5 3.9 %fusion.13 = bf16[2,96,384]{2,1,0:T(8,128)(2,1)S(1)} fusion(bf16[2,4096,384]{2,1,0:T(8,128)(2,1)} %param.23, f32[96,4224]{1,0:T(8,128)S(1)} %reshape.104, f32[2,96,384]{2,1,0:T(8,128)S(1)} %fusion.8), kind=kOutput, calls=%fused_computation.16 | convolution fusion | flops 604495872 | bytes 7520256 | tf_op jit(solution)/shard_map/ri,eif->erf/dot_general | solution.py:239
  79.5 2.0 %all_gather.14 = bf16[2,96,768]{2,1,0:T(8,128)(2,1)S(1)} all-gather(bf16[2,96,384]{2,1,0:T(8,128)(2,1)S(1)} %fusion.13), channel_id=1, replica_groups=mesh['parts'=2,'expert'=8,'group'=1,'tensor'=2] {'tensor'}, dimensions={2}, use_global_device_ids=true | all-gather | bytes 442368 | tf_op jit(solution)/shard_map/all_gather | solution.py:243
  81.6 4.0 %fusion.1 = bf16[96,2048]{1,0:T(8,128)(2,1)S(1)} fusion(bf16[2,96,768]{2,1,0:T(8,128)(2,1)S(1)} %all_gather.14, bf16[2,768,2048]{2,1,0:T(8,128)(2,1)} %param.24, f32[2,96]{1,0:T(2,128)S(1)} %copy.47), kind=kOutput, calls=%fused_computation.3 | convolution fusion | flops 604569600 | bytes 6980352 | tf_op jit(solution)/shard_map/erf,efo->ero/dot_general | solution.py:244
  85.6 0.9 convert_element_type.107
  86.5 3.5 %all-to-all-start = ((bf16[8,12,2048]{2,1,0:T(8,128)(2,1)}), bf16[8,12,2048]{2,1,0:T(8,128)(2,1)S(1)}, u32[]{:S(2)}, u32[]{:S(2)}) async-start(bf16[8,12,2048]{2,1,0:T(8,128)(2,1)} %convert_element_type.107), calls=%async_computation | async-start | bytes 1048576 | tf_op jit(solution)/shard_map/all_to_all | solution.py:247
  90.0 0.1 fusion.23
  90.2 0.1 reduce.1
  90.3 0.2 convert_reduce_fusion.1
  90.5 0.5 fusion.4
  91.0 0.2 slice_bitcast_fusion.23
  91.2 0.9 copy.50
  92.2 0.9 copy.51
  93.1 11.9 %all-to-all-done = bf16[8,12,2048]{2,1,0:T(8,128)(2,1)S(1)} async-done(((bf16[8,12,2048]{2,1,0:T(8,128)(2,1)}), bf16[8,12,2048]{2,1,0:T(8,128)(2,1)S(1)}, u32[]{:S(2)}, u32[]{:S(2)}) %all-to-all-start) | async-done | bytes 393248 | tf_op jit(solution)/shard_map/all_to_all | solution.py:247
  105.0 0.1 convert_reduce_fusion
  105.1 1.9 %all_gather.15 = bf16[12,4096]{1,0:T(8,128)(2,1)S(1)} all-gather(bf16[12,2048]{1,0:T(8,128)(2,1)S(1)} %add_convert_fusion), channel_id=1, replica_groups=mesh['parts'=2,'expert'=8,'group'=1,'tensor'=2] {'tensor'}, dimensions={1}, use_global_device_ids=true | all-gather | bytes 147456 | tf_op jit(solution)/shard_map/all_gather | solution.py:255
  107.0 0.7 reshape.99
  (42 shorter events, 0.9 us)
Async XLA Ops:
  7.2 2.0 %copy-start = (bf16[3,4,16,128]{3,2,1,0:T(8,128)(2,1)S(1)}, bf16[3,4,16,128]{3,2,1,0:T(8,128)(2,1)}, u32[]{:S(2)}) copy-start(bf16[3,4,16,128]{3,2,1,0:T(8,128)(2,1)} %param.14) | copy-start | bytes 147460
  7.2 62.8 %all-gather.3.cloned.1.call-start = ((), (), s32[]{:S(2)}) async-start(), calls=%async_computation.1 | async-start | bytes 2433024 | tf_op jit(solution)/shard_map/all_gather | solution.py:234
  8.0 4.2 %copy-start.3 = (bf16[3,4,4096]{2,1,0:T(4,128)(2,1)S(1)}, bf16[3,4,4096]{2,1,0:T(4,128)(2,1)}, u32[]{:S(2)}) copy-start(bf16[3,4,4096]{2,1,0:T(4,128)(2,1)} %param.13) | copy-start | bytes 294916
  9.2 3.3 %copy-start.6 = (f32[3,4,8]{2,1,0:T(4,128)S(1)}, f32[3,4,8]{2,1,0:T(4,128)}, u32[]{:S(2)}) copy-start(f32[3,4,8]{2,1,0:T(4,128)} %param.20) | copy-start | bytes 1156
  9.5 3.1 %copy-start.5 = (s32[3,4,8]{2,1,0:T(4,128)S(1)}, s32[3,4,8]{2,1,0:T(4,128)}, u32[]{:S(2)}) copy-start(s32[3,4,8]{2,1,0:T(4,128)} %param.19) | copy-start | bytes 1156
  9.5 3.2 %copy-start.7 = (s32[4]{0:T(128)S(1)}, s32[4]{0:T(128)}, u32[]{:S(2)}) copy-start(s32[4]{0:T(128)} %param.25) | copy-start | bytes 52
  9.5 3.3 %copy-start.4 = (f32[4096]{0:T(1024)S(1)}, f32[4096]{0:T(1024)}, u32[]{:S(2)}) copy-start(f32[4096]{0:T(1024)} %param.21) | copy-start | bytes 49156
  12.2 20.7 %copy-start.1 = (bf16[4,2,128,128]{3,2,1,0:T(8,128)(2,1)S(1)}, bf16[4,2,128,128]{3,2,1,0:T(8,128)(2,1)}, u32[]{:S(2)}) copy-start(bf16[4,2,128,128]{3,2,1,0:T(8,128)(2,1)} %param.18) | copy-start | bytes 786436
  12.3 20.6 %copy-start.2 = (bf16[4,2,128,128]{3,2,1,0:T(8,128)(2,1)S(1)}, bf16[4,2,128,128]{3,2,1,0:T(8,128)(2,1)}, u32[]{:S(2)}) copy-start(bf16[4,2,128,128]{3,2,1,0:T(8,128)(2,1)} %param.17) | copy-start | bytes 786436
  13.7 19.2 %collective-permute-start = (bf16[2,2,2,131,128]{4,3,2,1,0:T(8,128)(2,1)S(1)}, bf16[2,2,2,131,128]{4,3,2,1,0:T(8,128)(2,1)S(1)}, u32[]{:S(2)}, u32[]{:S(2)}) collective-permute-start(bf16[2,2,2,131,128]{4,3,2,1,0:T(8,128)(2,1)S(1)} %get-tuple-element.17), channel_id=1, source_target_pairs={{0,2},{2,4},{4,6},{6,8},{8,10},{10,12},{12,14},{1,3},{3,5},{5,7},{... | collective-permute-start | bytes 804872 | tf_op jit(solution)/shard_map/ppermute | solution.py:20
  18.4 14.5 %collective-permute-start.1 = (bf16[2,2,2,131,128]{4,3,2,1,0:T(8,128)(2,1)S(1)}, bf16[2,2,2,131,128]{4,3,2,1,0:T(8,128)(2,1)S(1)}, u32[]{:S(2)}, u32[]{:S(2)}) collective-permute-start(bf16[2,2,2,131,128]{4,3,2,1,0:T(8,128)(2,1)S(1)} %get-tuple-element.18), channel_id=1, source_target_pairs={{2,0},{4,2},{6,4},{8,6},{10,8},{12,10},{14,12},{3,1},{5,3},{7,5},{... | collective-permute-start | bytes 804872 | tf_op jit(solution)/shard_map/ppermute | solution.py:22
  86.5 18.5 %all-to-all-start = ((bf16[8,12,2048]{2,1,0:T(8,128)(2,1)}), bf16[8,12,2048]{2,1,0:T(8,128)(2,1)S(1)}, u32[]{:S(2)}, u32[]{:S(2)}) async-start(bf16[8,12,2048]{2,1,0:T(8,128)(2,1)} %convert_element_type.107), calls=%async_computation | async-start | bytes 1048576 | tf_op jit(solution)/shard_map/all_to_all | solution.py:247
Sparse Core Ops, SparseCore 0:
  13.7 56.1 all-gather.2
